TPU v7x, 32 devices: a whole 2x2x4 slice. The times are simulated.
32 devices in a mesh: region: 4 (over x, core), pair: 8 (over z, y).
Axes of the slice: x: 2, y: 2, z: 4, core: 2. Of those that a mesh axis runs over, the one named last changes fastest.
Arguments:
- points: float32 [3, 8192, 128], P(None, ('region', 'pair')), may hold values from -6 to 6
- offsets: float32 [3, 8192, 128], P(None, ('region', 'pair')), may hold values from -12 to 12
- normals: float32 [3, 8192, 128], P(None, ('region', 'pair')), may hold values from -6 to 6
- block_count: int32 [8192], P(('region', 'pair')), may hold values from 0 to 128, as said below
- block_edge: int32 [8192], P(('region', 'pair')), may hold values from 0 to 63
- edge_scan: int32 [2048], P(('region', 'pair')), may hold values from 0 to 127
- edge_nbr: int32 [2048], P(('region', 'pair')), may hold values from 0 to 383, as said below
- rotvec: float32 [3, 4096], P(None, ('region', 'pair')), may hold values from -0.3 to 0.3
Outputs:
- edge_pose: float32 [6, 2048], P(None, ('region', 'pair'))
- rotations: float32 [9, 4096], P(None, ('region', 'pair'))
Inputs may be any that keep to these rules, and one draw needn't show every extreme that they name: `block_count`: some block is full in every draw; a count of 0 marks an empty slot. `edge_nbr`: values below 128 name a scan of the device one step lower along region, values from 256 one of the device one step higher, the rest one of the device's own scans other than the slot's own scan; devices at the ends of region name no missing neighbour.
All inputs are finite; a program needn't handle non-finite values.
Results may differ from a plain program's by a relative error of at most 0.0003.
Values sent between devices are 32-bit elements; how exact they have to be, the bound alone decides.
A program may use at most 64 MiB of HBM per device.

v0:
```python
import functools
import math

import jax
import jax.numpy as jnp
from jax import lax
from jax.experimental import pallas as pl
from jax.experimental.pallas import tpu as pltpu
from jax.sharding import PartitionSpec as P

damping = 16.0
min_length = 0.1
MESH = pl.DeviceIdType.MESH
F32 = jnp.float32
BF16 = jnp.bfloat16
ROWS = 32


def far_first(count):
    return sorted(range(count), key=lambda d: (-min(d, count - d), d))


def exp_rotation(v):
    t = v[0] * v[0] + v[1] * v[1] + v[2] * v[2]
    a = 1.0 + t * (-1.0 / 6.0 + t * (1.0 / 120.0 + t * (-1.0 / 5040.0 + t * (1.0 / 362880.0))))
    b = 0.5 + t * (-1.0 / 24.0 + t * (1.0 / 720.0 + t * (-1.0 / 40320.0 + t * (1.0 / 3628800.0))))
    bv = [b * v[i] for i in range(3)]
    av = [a * v[i] for i in range(3)]
    diag = 1.0 - b * t
    xy, xz, yz = bv[0] * v[1], bv[0] * v[2], bv[1] * v[2]
    return [
        diag + bv[0] * v[0], xy - av[2], xz + av[1],
        xy + av[2], diag + bv[1] * v[1], yz - av[0],
        xz - av[1], yz + av[0], diag + bv[2] * v[2],
    ]


def angle(s, c):
    size = jnp.abs(c)
    big, small = jnp.maximum(s, size), jnp.minimum(s, size)
    far = small > 0.41421356 * big
    z = jnp.where(far, small - big, small) / jnp.maximum(jnp.where(far, small + big, big), 1e-30)
    z2 = z * z
    poly = ((8.05374449538e-2 * z2 - 1.38776856032e-1) * z2 + 1.99777106478e-1) * z2 - 3.33329491539e-1
    r = jnp.where(far, math.pi / 4, 0.0) + (z + z * z2 * poly)
    r = jnp.where(s > size, math.pi / 2 - r, r)
    return jnp.where(c < 0.0, math.pi - r, r)


def log_rotation(m):
    c = (m[0] + m[4] + m[8] - 1.0) * 0.5
    u = [0.5 * (m[7] - m[5]), 0.5 * (m[2] - m[6]), 0.5 * (m[3] - m[1])]
    s2 = u[0] * u[0] + u[1] * u[1] + u[2] * u[2]
    s = jnp.sqrt(s2)
    f = jnp.where(s < 0.0001, 1.0 + s2 / 6.0, angle(s, c) / jnp.maximum(s, 0.0001))
    return [f * x for x in u]


def mat_mul(x, y):
    return [sum(x[3 * a + b] * y[3 * b + c] for b in range(3)) for a in range(3) for c in range(3)]


def mat_tmul(x, y):
    return [sum(x[3 * b + a] * y[3 * b + c] for b in range(3)) for a in range(3) for c in range(3)]


def split_rows(x):
    hi = x.astype(BF16)
    rest = x - hi.astype(F32)
    mid = rest.astype(BF16)
    lo = (rest - mid.astype(F32)).astype(BF16)
    return jnp.concatenate([hi, mid, lo], axis=0)


def exact_dot(x, table, dims):
    rows = x.shape[0]
    out = lax.dot_general(split_rows(x), table, (dims, ((), ())), preferred_element_type=F32)
    return out[:rows] + out[rows : 2 * rows] + out[2 * rows :]


def one_hot(index, count, width):
    grid = lax.broadcasted_iota(jnp.int32, (count, width), 0)
    return jnp.where(grid == index, 1.0, 0.0).astype(BF16)


def solve(h, g):
    low = [[None] * 6 for _ in range(6)]
    val = [[None] * 6 for _ in range(6)]
    inv = [None] * 6
    for c in range(6):
        for r in range(c, 6):
            x = h[r][c]
            for k in range(c):
                x = x - val[r][k] * low[c][k]
            val[r][c] = x
        inv[c] = 1.0 / val[c][c]
        for r in range(c + 1, 6):
            low[r][c] = val[r][c] * inv[c]
    y = []
    for r in range(6):
        x = g[r]
        for k in range(r):
            x = x - low[r][k] * y[k]
        y.append(x)
    out = [None] * 6
    for r in range(5, -1, -1):
        x = y[r] * inv[r]
        for k in range(r + 1, 6):
            x = x - low[k][r] * out[k]
        out[r] = x
    return out


def kernel(
    sizes,
    pts_hbm, off_hbm, nrm_hbm, cnt_hbm, edge_hbm, scan_ref, nbr_ref, rv_ref,
    pose_ref, rot_ref,
    data, tr, tt, tab, send1, recv1, sums_ref, send2, recv2, rows2,
    rvh, sch, nbh, near_tab, own_tab, cnt_ref, edge_ref,
    in_sem, int_sem, s1, r1, s2, r2, hs, hr, es, er, ns, nr,
):
    regions, pairs, blocks, edges, scans = sizes
    n = regions * pairs
    slot = blocks // n
    per = edges // n
    per_row = 128 // ROWS
    m1 = slot * ROWS // 128
    ep = max(edges, 128)
    halves = blocks // 128
    reg, pair = lax.axis_index("region"), lax.axis_index("pair")
    me = reg * pairs + pair

    def wrapped(x, size):
        return jnp.where(x >= size, x - size, x)

    first_mid, mids = pairs // 4, pairs // 2
    is_mid = jnp.logical_and(pair >= first_mid, pair < first_mid + mids)
    taken = (reg * pairs + (pair - first_mid) * 2) * is_mid.astype(jnp.int32)
    beside = sorted({k % regions for k in (-2, -1, 1, 2)})

    def each_mid(send):
        def region_step(dr, carry):
            r = wrapped(reg + dr, regions)
            for i in range(mids):
                send(r * pairs + 2 * i, (r, first_mid + i))
            return carry

        if regions <= 4:
            for dr in range(1, regions):
                region_step(dr, 0)
        else:
            lax.fori_loop(1, regions, region_step, 0)
        for i in range(mids):
            @pl.when(pair != first_mid + i)
            def _():
                send(reg * pairs + 2 * i, (reg, first_mid + i))

    def each_other(send):
        def region_step(dr, carry):
            r = wrapped(reg + dr, regions)
            for dp in far_first(pairs):
                p = wrapped(pair + dp, pairs)
                send(r * pairs + p, (r, p))
            return carry

        lax.fori_loop(1, regions, region_step, 0)
        for dp in far_first(pairs)[:-1]:
            p = wrapped(pair + dp, pairs)
            send(reg * pairs + p, (reg, p))

    ints = [
        pltpu.make_async_copy(cnt_hbm, cnt_ref, int_sem.at[0]),
        pltpu.make_async_copy(edge_hbm, edge_ref, int_sem.at[1]),
    ]
    for copy in ints:
        copy.start()
    loads = []
    for h in range(halves):
        for a, ref in enumerate((pts_hbm, off_hbm, nrm_hbm)):
            copy = pltpu.make_async_copy(
                ref.at[:, pl.ds(h * 128, 128), :], data.at[h, a], in_sem.at[h, a]
            )
            copy.start()
            loads.append(copy)

    barrier = pltpu.get_barrier_semaphore()


    def greet(to, where):
        pl.semaphore_signal(barrier, inc=1, device_id=where, device_id_type=MESH)

    @pl.when(is_mid)
    def _():
        each_other(greet)

    @pl.when(jnp.logical_not(is_mid))
    def _():
        each_mid(greet)
        for dr in beside:
            r = wrapped(reg + dr, regions)
            greet(r, (r, pair))


    tt[...] = jnp.zeros_like(tt)
    rvh[pl.ds(5, 3)] = jnp.zeros((3, 3, scans), F32)
    rows2[...] = jnp.zeros_like(rows2)
    for copy in ints:
        copy.wait()
    for h in range(halves):
        for a in range(3):
            loads[3 * h + a].wait()
            for c in range(3):
                tr[3 * a + c] = data[h, a, c].T
        count = cnt_ref[:, h * 128 : (h + 1) * 128]

        def chunk(i, acc):
            acc = list(acc)
            for u in range(2):
                at = pl.multiple_of(i * 16 + u * 8, 8)
                p = [tr[c, pl.ds(at, 8), :] for c in range(3)]
                d = [tr[3 + c, pl.ds(at, 8), :] for c in range(3)]
                live = lax.broadcasted_iota(jnp.int32, (8, 128), 0) + at < count
                v = [jnp.where(live, tr[6 + c, pl.ds(at, 8), :], 0.0) for c in range(3)]
                jac = [
                    p[1] * v[2] - p[2] * v[1],
                    p[2] * v[0] - p[0] * v[2],
                    p[0] * v[1] - p[1] * v[0],
                ] + v
                resid = v[0] * d[0] + v[1] * d[1] + v[2] * d[2]
                at_t = 0
                for x in range(6):
                    for y in range(x + 1):
                        acc[at_t] = acc[at_t] + jac[x] * jac[y]
                        at_t += 1
                for x in range(6):
                    acc[21 + x] = acc[21 + x] + jac[x] * resid
            return tuple(acc)

        acc = lax.fori_loop(0, 8, chunk, tuple(jnp.zeros((8, 128), F32) for _ in range(27)))
        for t in range(27):
            tt[t : t + 1, :] = jnp.sum(acc[t], axis=0, keepdims=True)
        tt[27:28, :] = jnp.where(count > 0, 1.0, 0.0)
        tt[28:29, :] = edge_ref[:, h * 128 : (h + 1) * 128].astype(F32)
        tab[pl.ds(h * 128, 128), :] = tt[...].T
    for j in range(m1):
        row = tab[pl.ds(j * per_row, n, stride=slot), :]
        for k in range(1, per_row):
            row = row + pltpu.roll(tab[pl.ds(j * per_row + k, n, stride=slot), :], ROWS * k, 1)
        send1[:, j, :] = row

    @pl.when(is_mid)
    def _():
        pl.semaphore_wait(barrier, n - 1)

    @pl.when(jnp.logical_not(is_mid))
    def _():
        pl.semaphore_wait(barrier, regions * mids + len(beside))

    each_mid(
        lambda to, where: pltpu.make_async_remote_copy(
            send1.at[pl.ds(to, 2)], recv1.at[me], s1, r1, device_id=where, device_id_type=MESH
        ).start()
    )

    @pl.when(is_mid)
    def _():
        pltpu.make_async_copy(send1.at[pl.ds(taken, 2)], recv1.at[me], r1).start()


    for k in (-1, 1, -2, 2):
        where = (wrapped(reg + k % regions, regions), pair)
        pltpu.make_async_remote_copy(
            rv_ref, rvh.at[2 - k], hs, hr, device_id=where, device_id_type=MESH
        ).start()
        if abs(k) == 1:
            pltpu.make_async_remote_copy(
                scan_ref, sch.at[1 - k], es, er, device_id=where, device_id_type=MESH
            ).start()
            pltpu.make_async_remote_copy(
                nbr_ref, nbh.at[1 - k], ns, nr, device_id=where, device_id_type=MESH
            ).start()
    pltpu.make_async_copy(rv_ref, rvh.at[2], hr).start()
    pltpu.make_async_copy(scan_ref, sch.at[1], er).start()
    pltpu.make_async_copy(nbr_ref, nbh.at[1], nr).start()

    @pl.when(is_mid)
    def _():
        pltpu.make_async_copy(recv1, recv1, r1).wait()
        terms = []
        for half in range(2):
            got = [recv1[:, half, j, :] for j in range(m1)]
            wide = -(-(m1 * n) // 128) * 128
            if wide > m1 * n:
                got.append(jnp.zeros((wide - m1 * n, 128), F32))
            got = jnp.concatenate(got, axis=0)
            for i in range(wide // 128):
                part = got[128 * i : 128 * (i + 1)].T
                for k in range(per_row):
                    terms.append(part[ROWS * k : ROWS * (k + 1)])
        slots = lax.broadcasted_iota(jnp.int32, (edges, 64 * len(terms)), 0).astype(F32)
        both = []
        for half in range(2):
            mine = jnp.concatenate(terms[half * len(terms) // 2 : (half + 1) * len(terms) // 2], axis=1)
            table = jnp.where(slots == mine[28:29], 1.0, 0.0).astype(BF16)
            both.append(exact_dot(mine, table, ((1,), (1,))))
        sums_ref[...] = jnp.concatenate(both, axis=1)
        h, at_t = [[None] * 6 for _ in range(6)], 0
        for x in range(6):
            for y in range(x + 1):
                h[x][y] = sums_ref[at_t : at_t + 1, :] + (damping if x == y else 0.0)
                at_t += 1
        pose = [-x for x in solve(h, [sums_ref[21 + x : 22 + x, :] for x in range(6)])]
        payload = pose + [jnp.where(sums_ref[27:28, :] > 0.5, 1.0, 0.0)]
        stacked = jnp.concatenate(payload + [jnp.zeros((1, 2 * edges), F32)], axis=0)

        def turned(x, by):
            wide = x.shape[1]
            lane = lax.rem(lax.broadcasted_iota(jnp.int32, x.shape, 1), edges)
            one = pltpu.roll(x, by, 1)
            two = pltpu.roll(x, (by - edges) % wide, 1)
            return jnp.where(lane < by, two, one)

        lower = turned(stacked, per * pairs)
        upper = turned(stacked, edges - per * pairs)
        place = lax.broadcasted_iota(jnp.int32, (8, 2 * edges), 0)
        groups = []
        for t in range(7):
            groups.append(
                jnp.where(
                    place == 0,
                    lower[t : t + 1],
                    jnp.where(
                        place == 1, stacked[t : t + 1], jnp.where(place == 2, upper[t : t + 1], 0.0)
                    ),
                )
            )
        groups = jnp.concatenate(groups + [jnp.zeros((128 - 56, 2 * edges), F32)], axis=0)
        for i in range(2 * edges // 128):
            tab[pl.ds(128 * i, 128), :] = groups[:, 128 * i : 128 * (i + 1)].T
        for half in range(2):
            for j in range(per):
                send2[:, half, j, :] = tab[pl.ds(half * edges + j, n, stride=per), :]
        each_other(
            lambda to, where: pltpu.make_async_remote_copy(
                send2.at[to], recv2.at[pl.ds(taken, 2)], s2, r2, device_id=where, device_id_type=MESH
            ).start()
        )
        pltpu.make_async_copy(send2.at[me], recv2.at[pl.ds(taken, 2)], r2).start()

    pltpu.make_async_copy(rvh.at[pl.ds(0, 5)], rvh.at[pl.ds(0, 5)], hr).wait()
    pltpu.make_async_copy(sch, sch, er).wait()
    pltpu.make_async_copy(nbh, nbh, nr).wait()
    for q in range(3):
        near_tab[:, q * ep : q * ep + edges] = one_hot(nbh[q], 3 * scans, edges)
        own_tab[:, q * ep : q * ep + edges] = one_hot(sch[q], scans, edges)
        if ep > edges:
            near_tab[:, q * ep + edges : (q + 1) * ep] = jnp.zeros((3 * scans, ep - edges), BF16)
            own_tab[:, q * ep + edges : (q + 1) * ep] = jnp.zeros((scans, ep - edges), BF16)

    def up(x, k):
        return pltpu.roll(x, (8 - k) % 8, 0) if k % 8 else x

    def picked(out, c, sets, width):
        block = out[8 * c : 8 * c + 8]
        if len(sets) == 1:
            return block
        value = block[:, :width]
        for q in sets[1:]:
            value = jnp.where(
                lax.broadcasted_iota(jnp.int32, (8, width), 0) == q,
                block[:, q * width : (q + 1) * width],
                value,
            )
        return value

    def between(rot, sets, shift):
        cols = pl.ds(sets[0] * ep, len(sets) * ep)
        parts = [
            jnp.concatenate([up(x, s + shift) for x in rot], axis=0) for s in range(3)
        ]
        near = exact_dot(jnp.concatenate(parts, axis=1), near_tab[:, cols], ((1,), (0,)))
        mine = exact_dot(parts[1], own_tab[:, cols], ((1,), (0,)))
        return mat_tmul(
            [picked(mine, c, sets, ep) for c in range(9)],
            [picked(near, c, sets, ep) for c in range(9)],
        )

    def step(rot, link, relative, live, sets):
        cols = pl.ds(sets[0] * ep, len(sets) * ep)
        tangent = log_rotation(mat_mul(link, relative))
        length = jnp.sqrt(tangent[0] * tangent[0] + tangent[1] * tangent[1] + tangent[2] * tangent[2])
        weight = live / jnp.maximum(length, min_length)
        weighed = jnp.concatenate([weight * x for x in tangent] + [weight], axis=0)
        parts = [
            exact_dot(weighed, own_tab[:, pl.ds(q * ep, ep)], ((1,), (1,))) for q in sets
        ]
        total = jnp.concatenate(parts, axis=1)
        numer = [picked(total, c, sets, scans) for c in range(3)]
        scale = 1.0 / (picked(total, 3, sets, scans) + 1.0)
        return mat_mul(rot, exp_rotation([x * scale for x in numer]))

    first = exp_rotation([rvh[:, c, :] for c in range(3)])
    everyone = (0, 1, 2)
    link = between(first, everyone, 0)
    base = [up(x, 1) for x in first]

    pltpu.make_async_copy(recv2, recv2, r2).wait()
    for j in range(per):
        rows2[pl.ds(j, n, stride=per), :] = recv2[:, j, :]
    back = [rows2[pl.ds(128 * i, 128), :].T for i in range(ep // 128)]
    back = jnp.concatenate(back, axis=1) if len(back) > 1 else back[0]
    comp = [back[8 * t : 8 * t + 8] for t in range(7)]
    for t in range(6):
        pose_ref[t : t + 1, :] = comp[t][1:2, :edges]
    relative = exp_rotation(comp[:3])
    second = step(base, link, relative, comp[6], everyone)
    link = between(second, (1,), -1)
    final = step(second, link, relative, comp[6], (1,))
    for c in range(9):
        rot_ref[c : c + 1, :] = final[c][1:2]

    @pl.when(is_mid)
    def _():
        sent = send1.at[pl.ds(0, n - 2)]
        pltpu.make_async_copy(sent, sent, s1).wait()
        sent = send2.at[pl.ds(0, n - 1)]
        pltpu.make_async_copy(sent, sent, s2).wait()

    @pl.when(jnp.logical_not(is_mid))
    def _():
        pltpu.make_async_copy(send1, send1, s1).wait()

    pltpu.make_async_copy(rvh.at[pl.ds(0, 4)], rvh.at[pl.ds(0, 4)], hs).wait()
    pltpu.make_async_copy(sch.at[pl.ds(0, 2)], sch.at[pl.ds(0, 2)], es).wait()
    pltpu.make_async_copy(nbh.at[pl.ds(0, 2)], nbh.at[pl.ds(0, 2)], ns).wait()


def finish(pose_ref, rot_ref, pose_out, rot_out, sems):
    copies = [
        pltpu.make_async_copy(pose_ref, pose_out, sems.at[0]),
        pltpu.make_async_copy(rot_ref, rot_out, sems.at[1]),
    ]
    for copy in copies:
        copy.start()
    for copy in copies:
        copy.wait()


def solution(mesh):
    regions, pairs = mesh.shape["region"], mesh.shape["pair"]
    n = regions * pairs

    def on_device(points, offsets, normals, block_count, block_edge, edge_scan, edge_nbr, rotvec):
        blocks, edges, scans = points.shape[1], edge_scan.shape[0], rotvec.shape[1]
        slot, per = blocks // n, edges // n
        m1 = slot * ROWS // 128
        ep = max(edges, 128)
        dma = pltpu.SemaphoreType.DMA
        vm = pl.BlockSpec(memory_space=pltpu.VMEM)
        hbm = pl.BlockSpec(memory_space=pl.ANY)
        pose, rot = pl.pallas_call(
            functools.partial(kernel, (regions, pairs, blocks, edges, scans)),
            out_shape=(pltpu.VMEM((6, edges), F32), pltpu.VMEM((9, scans), F32)),
            in_specs=[hbm] * 8,
            out_specs=(vm, vm),
            scratch_shapes=[
                pltpu.VMEM((blocks // 128, 3, 3, 128, 128), F32),
                pltpu.VMEM((9, 128, 128), F32),
                pltpu.VMEM((128, 128), F32),
                pltpu.VMEM((max(blocks, 2 * edges), 128), F32),
                pltpu.VMEM((n, m1, 128), F32),
                pltpu.VMEM((n, 2, m1, 128), F32),
                pltpu.VMEM((ROWS, 2 * edges), F32),
                pltpu.VMEM((n, 2, per, 128), F32),
                pltpu.VMEM((n, per, 128), F32),
                pltpu.VMEM((ep, 128), F32),
                pltpu.VMEM((8, 3, scans), F32),
                pltpu.VMEM((3, 1, edges), jnp.int32),
                pltpu.VMEM((3, 1, edges), jnp.int32),
                pltpu.VMEM((3 * scans, 3 * ep), BF16),
                pltpu.VMEM((scans, 3 * ep), BF16),
                pltpu.VMEM((1, blocks), jnp.int32),
                pltpu.VMEM((1, blocks), jnp.int32),
                dma((blocks // 128, 3)),
                dma((2,)),
                dma, dma, dma, dma, dma, dma, dma, dma, dma, dma,
            ],
            compiler_params=pltpu.CompilerParams(collective_id=0, has_side_effects=True),
        )(
            points, offsets, normals, block_count[None], block_edge[None],
            edge_scan[None], edge_nbr[None], rotvec,
        )
        return pl.pallas_call(
            finish,
            out_shape=(
                jax.ShapeDtypeStruct((6, edges), F32),
                jax.ShapeDtypeStruct((9, scans), F32),
            ),
            in_specs=[vm] * 2,
            out_specs=(hbm, hbm),
            scratch_shapes=[dma((2,))],
        )(*(pltpu.with_memory_space_constraint(x, pltpu.VMEM) for x in (pose, rot)))

    flat = P(("region", "pair"))
    cut = P(None, ("region", "pair"))
    return jax.shard_map(
        on_device,
        mesh=mesh,
        in_specs=(P(None, ("region", "pair"), None),) * 3 + (flat,) * 4 + (cut,),
        out_specs=(cut, cut),
        check_vma=False,
    )
```

profile of v0, /device:TPU:0, one launch (start us, length us, event | category | flops | bytes accessed | tf_op | source)
XLA Modules:
  0.0 17.1 jit_solution(15659769951459167675)
XLA Ops:
  0.6 15.9 %shard_map.95 = (f32[6,64]{1,0:T(8,128)S(1)}, f32[9,128]{1,0:T(8,128)S(1)}) custom-call(f32[3,256,128]{2,1,0:T(8,128)} %pts_hbm.1, f32[3,256,128]{2,1,0:T(8,128)} %off_hbm.1, f32[3,256,128]{2,1,0:T(8,128)} %nrm_hbm.1, s32[1,256]{1,0:T(1,128)} %bitcast.4, s32[1,256]{1,0:T(1,128)} %bitcast.5, s32[1,64]{1,0:T(1,128)} %bitcast.6, s32[1,64]{1,0:T(1,128)} %bitcast.7, ...), custom_call_target="tpu_custom_call" | custom-call | tf_op jit(solution)/shard_map/pallas_call | solution.py:461
  16.5 0.6 %shard_map.96 = (f32[6,64]{1,0:T(8,128)}, f32[9,128]{1,0:T(8,128)}) custom-call(f32[6,64]{1,0:T(8,128)S(1)} %get-tuple-element.4.pose_ref, f32[9,128]{1,0:T(8,128)S(1)} %get-tuple-element.5.rot_ref), custom_call_target="tpu_custom_call" | custom-call | tf_op jit(solution)/shard_map/pallas_call | solution.py:493
where the time goes:
time: 17.3 us; the launch traced here: 17.1 us
  Pallas kernels  16.5 us (95%)
  between operations  0.64 us (4%)
    pallas_call x1, Pallas kernels, on_device(): pl.pallas_call(functools.partial(kernel, (regions, pairs, blocks, edges,...  15.9 us
    pallas_call x1, Pallas kernels, on_device(): pl.pallas_call(finish, out_shape=(jax.ShapeDtypeStruct((6, edges), F32),...  0.62 us

commit v1 on v0

--- a/solution.py
+++ b/solution.py
@@ -14,10 +14,15 @@
 F32 = jnp.float32
 BF16 = jnp.bfloat16
 ROWS = 32
-
-
-def far_first(count):
-    return sorted(range(count), key=lambda d: (-min(d, count - d), d))
+KEPT = 4
+
+
+def owners(regions, pairs):
+    near = sorted(
+        ((r, p) for r in range(regions) for p in range(pairs)),
+        key=lambda at: (at[0] // 2 + at[1] // 2 + at[1] % 2, at[0] // 2, at[1], at[0]),
+    )
+    return sorted(near[: regions * pairs // KEPT])
 
 
 def exp_rotation(v):
@@ -64,18 +69,16 @@
     return [sum(x[3 * b + a] * y[3 * b + c] for b in range(3)) for a in range(3) for c in range(3)]
 
 
-def split_rows(x):
+def split_pair(x):
     hi = x.astype(BF16)
-    rest = x - hi.astype(F32)
-    mid = rest.astype(BF16)
-    lo = (rest - mid.astype(F32)).astype(BF16)
-    return jnp.concatenate([hi, mid, lo], axis=0)
+    mid = (x - hi.astype(F32)).astype(BF16)
+    return jnp.concatenate([hi, mid], axis=0)
 
 
 def exact_dot(x, table, dims):
     rows = x.shape[0]
-    out = lax.dot_general(split_rows(x), table, (dims, ((), ())), preferred_element_type=F32)
-    return out[:rows] + out[rows : 2 * rows] + out[2 * rows :]
+    out = lax.dot_general(split_pair(x), table, (dims, ((), ())), preferred_element_type=F32)
+    return out[:rows] + out[rows:]
 
 
 def one_hot(index, count, width):
@@ -115,7 +118,7 @@
     sizes,
     pts_hbm, off_hbm, nrm_hbm, cnt_hbm, edge_hbm, scan_ref, nbr_ref, rv_ref,
     pose_ref, rot_ref,
-    data, tr, tt, tab, send1, recv1, sums_ref, send2, recv2, rows2,
+    data, tr, tt, tab, send1, recv1, sums_ref, poses, groups, send2, recv2, rows2,
     rvh, sch, nbh, near_tab, own_tab, cnt_ref, edge_ref,
     in_sem, int_sem, s1, r1, s2, r2, hs, hr, es, er, ns, nr,
 ):
@@ -133,40 +136,41 @@
     def wrapped(x, size):
         return jnp.where(x >= size, x - size, x)
 
-    first_mid, mids = pairs // 4, pairs // 2
-    is_mid = jnp.logical_and(pair >= first_mid, pair < first_mid + mids)
-    taken = (reg * pairs + (pair - first_mid) * 2) * is_mid.astype(jnp.int32)
+    mids = owners(regions, pairs)
+
+    def holds(r, p):
+        hit = [jnp.logical_and(r == a, p == b) for a, b in mids]
+        return functools.reduce(jnp.logical_or, hit)
+
+    is_mid = holds(reg, pair)
+    rank = sum(jnp.where(me == r * pairs + p, k, 0) for k, (r, p) in enumerate(mids))
     beside = sorted({k % regions for k in (-2, -1, 1, 2)})
 
     def each_mid(send):
-        def region_step(dr, carry):
-            r = wrapped(reg + dr, regions)
-            for i in range(mids):
-                send(r * pairs + 2 * i, (r, first_mid + i))
-            return carry
-
-        if regions <= 4:
-            for dr in range(1, regions):
-                region_step(dr, 0)
-        else:
-            lax.fori_loop(1, regions, region_step, 0)
-        for i in range(mids):
-            @pl.when(pair != first_mid + i)
-            def _():
-                send(reg * pairs + 2 * i, (reg, first_mid + i))
+        @pl.when(is_mid)
+        def _():
+            for k, where in enumerate(mids):
+                @pl.when(rank != k)
+                def _():
+                    send(k, where)
+
+        @pl.when(jnp.logical_not(is_mid))
+        def _():
+            for k, where in enumerate(mids):
+                send(k, where)
 
     def each_other(send):
-        def region_step(dr, carry):
-            r = wrapped(reg + dr, regions)
-            for dp in far_first(pairs):
-                p = wrapped(pair + dp, pairs)
+        def step(dp, carry):
+            p = wrapped(pair + pairs - dp, pairs)
+            for dr in range(regions):
+                r = wrapped(reg + dr, regions)
                 send(r * pairs + p, (r, p))
             return carry
 
-        lax.fori_loop(1, regions, region_step, 0)
-        for dp in far_first(pairs)[:-1]:
-            p = wrapped(pair + dp, pairs)
-            send(reg * pairs + p, (reg, p))
+        for dr in range(1, regions):
+            r = wrapped(reg + dr, regions)
+            send(r * pairs + pair, (r, pair))
+        lax.fori_loop(1, pairs, step, 0)
 
     ints = [
         pltpu.make_async_copy(cnt_hbm, cnt_ref, int_sem.at[0]),
@@ -189,18 +193,25 @@
     def greet(to, where):
         pl.semaphore_signal(barrier, inc=1, device_id=where, device_id_type=MESH)
 
+    sides = [wrapped(reg + dr, regions) for dr in beside]
+    apart = [jnp.logical_not(holds(r, pair)) for r in sides]
+
     @pl.when(is_mid)
     def _():
         each_other(greet)
 
     @pl.when(jnp.logical_not(is_mid))
     def _():
-        each_mid(greet)
-        for dr in beside:
-            r = wrapped(reg + dr, regions)
-            greet(r, (r, pair))
-
-
+        for r, p in mids:
+            greet(r * pairs + p, (r, p))
+        for r, other in zip(sides, apart):
+            @pl.when(other)
+            def _():
+                greet(r, (r, pair))
+
+    groups[...] = jnp.zeros_like(groups)
+    poses[...] = jnp.zeros_like(poses)
+    sums_ref[...] = jnp.zeros_like(sums_ref)
     tt[...] = jnp.zeros_like(tt)
     rvh[pl.ds(5, 3)] = jnp.zeros((3, 3, scans), F32)
     rows2[...] = jnp.zeros_like(rows2)
@@ -254,18 +265,17 @@
 
     @pl.when(jnp.logical_not(is_mid))
     def _():
-        pl.semaphore_wait(barrier, regions * mids + len(beside))
+        pl.semaphore_wait(barrier, len(mids) + sum(other.astype(jnp.int32) for other in apart))
 
     each_mid(
-        lambda to, where: pltpu.make_async_remote_copy(
-            send1.at[pl.ds(to, 2)], recv1.at[me], s1, r1, device_id=where, device_id_type=MESH
+        lambda k, where: pltpu.make_async_remote_copy(
+            send1.at[pl.ds(k * KEPT, KEPT)], recv1.at[me], s1, r1, device_id=where, device_id_type=MESH
         ).start()
     )
 
     @pl.when(is_mid)
     def _():
-        pltpu.make_async_copy(send1.at[pl.ds(taken, 2)], recv1.at[me], r1).start()
-
+        pltpu.make_async_copy(send1.at[pl.ds(rank * KEPT, KEPT)], recv1.at[me], r1).start()
 
     for k in (-1, 1, -2, 2):
         where = (wrapped(reg + k % regions, regions), pair)
@@ -286,66 +296,93 @@
     @pl.when(is_mid)
     def _():
         pltpu.make_async_copy(recv1, recv1, r1).wait()
-        terms = []
-        for half in range(2):
-            got = [recv1[:, half, j, :] for j in range(m1)]
-            wide = -(-(m1 * n) // 128) * 128
-            if wide > m1 * n:
-                got.append(jnp.zeros((wide - m1 * n, 128), F32))
+        wide = max(edges, 128)
+        span = wide // edges
+        lanes = m1 * n
+        for q in range(KEPT // span):
+            got = [recv1[:, q * span + h, j, :] for h in range(span) for j in range(m1)]
             got = jnp.concatenate(got, axis=0)
+            turned_rows = [got[128 * i : 128 * (i + 1)].T for i in range(span * lanes // 128)]
+            turned_rows = jnp.concatenate(turned_rows, axis=1) if len(turned_rows) > 1 else turned_rows[0]
+            mine = [turned_rows[ROWS * k : ROWS * (k + 1)] for k in range(per_row)]
+            owner = lax.broadcasted_iota(jnp.int32, (1, span * lanes), 1) // lanes * edges
+            offset = owner.astype(F32)
+            slots = lax.broadcasted_iota(jnp.int32, (wide, span * lanes), 0).astype(F32)
+            table = [jnp.where(slots == x[28:29] + offset, 1.0, 0.0).astype(BF16) for x in mine]
+            total = exact_dot(
+                jnp.concatenate(mine, axis=1), jnp.concatenate(table, axis=1), ((1,), (1,))
+            )
             for i in range(wide // 128):
-                part = got[128 * i : 128 * (i + 1)].T
-                for k in range(per_row):
-                    terms.append(part[ROWS * k : ROWS * (k + 1)])
-        slots = lax.broadcasted_iota(jnp.int32, (edges, 64 * len(terms)), 0).astype(F32)
-        both = []
-        for half in range(2):
-            mine = jnp.concatenate(terms[half * len(terms) // 2 : (half + 1) * len(terms) // 2], axis=1)
-            table = jnp.where(slots == mine[28:29], 1.0, 0.0).astype(BF16)
-            both.append(exact_dot(mine, table, ((1,), (1,))))
-        sums_ref[...] = jnp.concatenate(both, axis=1)
+                sums_ref[pl.ds(q * (wide // 128) + i, ROWS, stride=8), :] = total[:, 128 * i : 128 * (i + 1)]
+        sets = KEPT * edges // 128
         h, at_t = [[None] * 6 for _ in range(6)], 0
         for x in range(6):
             for y in range(x + 1):
-                h[x][y] = sums_ref[at_t : at_t + 1, :] + (damping if x == y else 0.0)
+                h[x][y] = sums_ref[8 * at_t : 8 * at_t + 8, :] + (damping if x == y else 0.0)
                 at_t += 1
-        pose = [-x for x in solve(h, [sums_ref[21 + x : 22 + x, :] for x in range(6)])]
-        payload = pose + [jnp.where(sums_ref[27:28, :] > 0.5, 1.0, 0.0)]
-        stacked = jnp.concatenate(payload + [jnp.zeros((1, 2 * edges), F32)], axis=0)
+        pose = [-x for x in solve(h, [sums_ref[8 * (21 + x) : 8 * (22 + x), :] for x in range(6)])]
+        payload = pose + [jnp.where(sums_ref[8 * 27 : 8 * 28, :] > 0.5, 1.0, 0.0)]
+        for t in range(7):
+            poses[1, sets * t : sets * (t + 1), :] = payload[t][:sets]
+        stacked = poses[1]
 
         def turned(x, by):
-            wide = x.shape[1]
-            lane = lax.rem(lax.broadcasted_iota(jnp.int32, x.shape, 1), edges)
-            one = pltpu.roll(x, by, 1)
-            two = pltpu.roll(x, (by - edges) % wide, 1)
-            return jnp.where(lane < by, two, one)
-
-        lower = turned(stacked, per * pairs)
-        upper = turned(stacked, edges - per * pairs)
-        place = lax.broadcasted_iota(jnp.int32, (8, 2 * edges), 0)
-        groups = []
-        for t in range(7):
-            groups.append(
-                jnp.where(
-                    place == 0,
-                    lower[t : t + 1],
-                    jnp.where(
-                        place == 1, stacked[t : t + 1], jnp.where(place == 2, upper[t : t + 1], 0.0)
-                    ),
+            if edges <= 128:
+                lane = lax.rem(lax.broadcasted_iota(jnp.int32, x.shape, 1), edges)
+                one = pltpu.roll(x, by, 1)
+                two = pltpu.roll(x, (by - edges) % 128, 1)
+                return jnp.where(lane < by, two, one)
+            part = edges // 128
+            row = lax.rem(lax.broadcasted_iota(jnp.int32, x.shape, 0), part)
+            tall = x.shape[0]
+
+            def moved(k):
+                back = k % part
+                if back == 0:
+                    return x
+                return jnp.where(
+                    row >= back, pltpu.roll(x, back, 0), pltpu.roll(x, (back - part) % tall, 0)
                 )
+
+            lane = lax.broadcasted_iota(jnp.int32, x.shape, 1)
+            whole, rest = by // 128, by % 128
+            if rest == 0:
+                return moved(whole)
+            return jnp.where(
+                lane < rest, pltpu.roll(moved(whole + 1), rest, 1), pltpu.roll(moved(whole), rest, 1)
             )
-        groups = jnp.concatenate(groups + [jnp.zeros((128 - 56, 2 * edges), F32)], axis=0)
-        for i in range(2 * edges // 128):
-            tab[pl.ds(128 * i, 128), :] = groups[:, 128 * i : 128 * (i + 1)].T
-        for half in range(2):
-            for j in range(per):
-                send2[:, half, j, :] = tab[pl.ds(half * edges + j, n, stride=per), :]
+
+        poses[0] = turned(stacked, per * pairs)
+        poses[2] = turned(stacked, edges - per * pairs)
+        for q in range(sets):
+            for g in range(3):
+                groups[q, pl.ds(g, 8, stride=4), :] = poses[g, pl.ds(q, 8, stride=sets), :]
+        held = 128 // ROWS
+        for q in range(0, sets, held):
+            some = range(q, min(q + held, sets))
+            flat = jnp.concatenate([groups[i] for i in some], axis=0)
+            if len(some) < held:
+                flat = jnp.concatenate([flat, jnp.zeros((128 - ROWS * len(some), 128), F32)], axis=0)
+            tab[pl.ds(128 * (q // held), 128), :] = flat.T
+        for j in range(per):
+            if edges <= 128:
+                row = tab[pl.ds(j, n, stride=per), :]
+                for h2 in range(1, span):
+                    row = row + pltpu.roll(tab[pl.ds(h2 * edges + j, n, stride=per), :], ROWS * sets * h2, 1)
+                send2[:, j, 0, :] = row
+            else:
+                part = edges // 128
+                count = 128 // per
+                for i in range(sets // held):
+                    block = tab[pl.ds(128 * i + j, count, stride=per), :]
+                    for b in range(part):
+                        send2[pl.ds(b * count, count), j, i, :] = pltpu.roll(block, (128 - ROWS * b) % 128, 1)
         each_other(
             lambda to, where: pltpu.make_async_remote_copy(
-                send2.at[to], recv2.at[pl.ds(taken, 2)], s2, r2, device_id=where, device_id_type=MESH
+                send2.at[to], recv2.at[rank], s2, r2, device_id=where, device_id_type=MESH
             ).start()
         )
-        pltpu.make_async_copy(send2.at[me], recv2.at[pl.ds(taken, 2)], r2).start()
+        pltpu.make_async_copy(send2.at[me], recv2.at[rank], r2).start()
 
     pltpu.make_async_copy(rvh.at[pl.ds(0, 5)], rvh.at[pl.ds(0, 5)], hr).wait()
     pltpu.make_async_copy(sch, sch, er).wait()
@@ -405,11 +442,22 @@
     base = [up(x, 1) for x in first]
 
     pltpu.make_async_copy(recv2, recv2, r2).wait()
-    for j in range(per):
-        rows2[pl.ds(j, n, stride=per), :] = recv2[:, j, :]
+    part = max(edges // 128, 1)
+    span = max(128 // edges, 1)
+    sets = KEPT * edges // 128
+    for o in range(KEPT):
+        lane, row = (ROWS * (o % span * sets + o // span), 0) if edges <= 128 else (ROWS * part * o, 0)
+        row, lane = lane // 128, lane % 128
+        for j in range(per):
+            rows2[pl.ds(per * o + j, len(mids), stride=per * KEPT), :] = pltpu.roll(
+                recv2[:, j, row, :], (128 - lane) % 128, 1
+            ) if lane else recv2[:, j, row, :]
     back = [rows2[pl.ds(128 * i, 128), :].T for i in range(ep // 128)]
     back = jnp.concatenate(back, axis=1) if len(back) > 1 else back[0]
-    comp = [back[8 * t : 8 * t + 8] for t in range(7)]
+    comp = []
+    for t in range(7):
+        block = back[8 * (t // 2) : 8 * (t // 2) + 8]
+        comp.append(pltpu.roll(block, 4, 0) if t % 2 else block)
     for t in range(6):
         pose_ref[t : t + 1, :] = comp[t][1:2, :edges]
     relative = exp_rotation(comp[:3])
@@ -421,7 +469,7 @@
 
     @pl.when(is_mid)
     def _():
-        sent = send1.at[pl.ds(0, n - 2)]
+        sent = send1.at[pl.ds(0, n - KEPT)]
         pltpu.make_async_copy(sent, sent, s1).wait()
         sent = send2.at[pl.ds(0, n - 1)]
         pltpu.make_async_copy(sent, sent, s2).wait()
@@ -455,6 +503,8 @@
         slot, per = blocks // n, edges // n
         m1 = slot * ROWS // 128
         ep = max(edges, 128)
+        sets = KEPT * edges // 128
+        lines = max(edges // 128, 1)
         dma = pltpu.SemaphoreType.DMA
         vm = pl.BlockSpec(memory_space=pltpu.VMEM)
         hbm = pl.BlockSpec(memory_space=pl.ANY)
@@ -467,12 +517,14 @@
                 pltpu.VMEM((blocks // 128, 3, 3, 128, 128), F32),
                 pltpu.VMEM((9, 128, 128), F32),
                 pltpu.VMEM((128, 128), F32),
-                pltpu.VMEM((max(blocks, 2 * edges), 128), F32),
+                pltpu.VMEM((max(blocks, KEPT * edges), 128), F32),
                 pltpu.VMEM((n, m1, 128), F32),
-                pltpu.VMEM((n, 2, m1, 128), F32),
-                pltpu.VMEM((ROWS, 2 * edges), F32),
-                pltpu.VMEM((n, 2, per, 128), F32),
-                pltpu.VMEM((n, per, 128), F32),
+                pltpu.VMEM((n, KEPT, m1, 128), F32),
+                pltpu.VMEM((8 * ROWS, 128), F32),
+                pltpu.VMEM((3, 8 * sets, 128), F32),
+                pltpu.VMEM((sets, ROWS, 128), F32),
+                pltpu.VMEM((n, per, lines, 128), F32),
+                pltpu.VMEM((n // KEPT, per, lines, 128), F32),
                 pltpu.VMEM((ep, 128), F32),
                 pltpu.VMEM((8, 3, scans), F32),
                 pltpu.VMEM((3, 1, edges), jnp.int32),

time: 17.3 us -> 16.8 us (0.971)
  Pallas kernels: 16.5 us -> 16.1 us
    pallas_call x1, Pallas kernels: 15.9 us -> 15.4 us  [on_device(): pl.pallas_call(functools.partial(kernel, (regions, pairs, blocks, edges,...]
where the time goes in v1:
time: 16.8 us; the launch traced here: 16.7 us
  Pallas kernels  16.1 us (96%)
  between operations  0.64 us (4%)
    pallas_call x1, Pallas kernels, on_device(): pl.pallas_call(functools.partial(kernel, (regions, pairs, blocks, edges,...  15.4 us
    pallas_call x1, Pallas kernels, on_device(): pl.pallas_call(finish, out_shape=(jax.ShapeDtypeStruct((6, edges), F32),...  0.62 us

profile of v1, /device:TPU:0, one launch (start us, length us, event | category | flops | bytes accessed | tf_op | source)
XLA Modules:
  0.0 16.7 jit_solution(17886169851251794342)
XLA Ops:
  0.6 15.4 %shard_map.95 = (f32[6,64]{1,0:T(8,128)S(1)}, f32[9,128]{1,0:T(8,128)S(1)}) custom-call(f32[3,256,128]{2,1,0:T(8,128)} %pts_hbm.1, f32[3,256,128]{2,1,0:T(8,128)} %off_hbm.1, f32[3,256,128]{2,1,0:T(8,128)} %nrm_hbm.1, s32[1,256]{1,0:T(1,128)} %bitcast.4, s32[1,256]{1,0:T(1,128)} %bitcast.5, s32[1,64]{1,0:T(1,128)} %bitcast.6, s32[1,64]{1,0:T(1,128)} %bitcast.7, ...), custom_call_target="tpu_custom_call" | custom-call | tf_op jit(solution)/shard_map/pallas_call | solution.py:511
  16.1 0.6 %shard_map.96 = (f32[6,64]{1,0:T(8,128)}, f32[9,128]{1,0:T(8,128)}) custom-call(f32[6,64]{1,0:T(8,128)S(1)} %get-tuple-element.4.pose_ref, f32[9,128]{1,0:T(8,128)S(1)} %get-tuple-element.5.rot_ref), custom_call_target="tpu_custom_call" | custom-call | tf_op jit(solution)/shard_map/pallas_call | solution.py:545

commit v2 on v1

--- a/solution.py
+++ b/solution.py
@@ -212,51 +212,57 @@
     groups[...] = jnp.zeros_like(groups)
     poses[...] = jnp.zeros_like(poses)
     sums_ref[...] = jnp.zeros_like(sums_ref)
-    tt[...] = jnp.zeros_like(tt)
+    tt[pl.ds(8 * 27, 8 * 5), :] = jnp.zeros((8 * 5, 128), F32)
     rvh[pl.ds(5, 3)] = jnp.zeros((3, 3, scans), F32)
     rows2[...] = jnp.zeros_like(rows2)
     for copy in ints:
         copy.wait()
+    def turn(h, i):
+        tr[h % 2, i] = data[h, i // 3, i % 3].T
+
+    def chunk(h, at, acc):
+        p = [tr[h % 2, c, pl.ds(at, 8), :] for c in range(3)]
+        d = [tr[h % 2, 3 + c, pl.ds(at, 8), :] for c in range(3)]
+        live = lax.broadcasted_iota(jnp.int32, (8, 128), 0) + at < cnt_ref[:, h * 128 : (h + 1) * 128]
+        v = [jnp.where(live, tr[h % 2, 6 + c, pl.ds(at, 8), :], 0.0) for c in range(3)]
+        jac = [
+            p[1] * v[2] - p[2] * v[1],
+            p[2] * v[0] - p[0] * v[2],
+            p[0] * v[1] - p[1] * v[0],
+        ] + v
+        resid = v[0] * d[0] + v[1] * d[1] + v[2] * d[2]
+        new = [jac[x] * jac[y] for x in range(6) for y in range(x + 1)] + [x * resid for x in jac]
+        return [a + b for a, b in zip(acc, new)] if acc else new
+
+    for a in range(3):
+        loads[a].wait()
+        for c in range(3):
+            turn(0, 3 * a + c)
     for h in range(halves):
-        for a in range(3):
-            loads[3 * h + a].wait()
-            for c in range(3):
-                tr[3 * a + c] = data[h, a, c].T
-        count = cnt_ref[:, h * 128 : (h + 1) * 128]
-
-        def chunk(i, acc):
-            acc = list(acc)
-            for u in range(2):
-                at = pl.multiple_of(i * 16 + u * 8, 8)
-                p = [tr[c, pl.ds(at, 8), :] for c in range(3)]
-                d = [tr[3 + c, pl.ds(at, 8), :] for c in range(3)]
-                live = lax.broadcasted_iota(jnp.int32, (8, 128), 0) + at < count
-                v = [jnp.where(live, tr[6 + c, pl.ds(at, 8), :], 0.0) for c in range(3)]
-                jac = [
-                    p[1] * v[2] - p[2] * v[1],
-                    p[2] * v[0] - p[0] * v[2],
-                    p[0] * v[1] - p[1] * v[0],
-                ] + v
-                resid = v[0] * d[0] + v[1] * d[1] + v[2] * d[2]
-                at_t = 0
-                for x in range(6):
-                    for y in range(x + 1):
-                        acc[at_t] = acc[at_t] + jac[x] * jac[y]
-                        at_t += 1
-                for x in range(6):
-                    acc[21 + x] = acc[21 + x] + jac[x] * resid
-            return tuple(acc)
-
-        acc = lax.fori_loop(0, 8, chunk, tuple(jnp.zeros((8, 128), F32) for _ in range(27)))
+        more = h + 1 < halves
+        if more:
+            for a in range(3):
+                loads[3 * h + 3 + a].wait()
+        acc, done = [], 0
+        for i in range(16):
+            acc = chunk(h, 8 * i, acc)
+            while more and done * 16 < 9 * (i + 1):
+                turn(h + 1, done)
+                done += 1
         for t in range(27):
-            tt[t : t + 1, :] = jnp.sum(acc[t], axis=0, keepdims=True)
-        tt[27:28, :] = jnp.where(count > 0, 1.0, 0.0)
-        tt[28:29, :] = edge_ref[:, h * 128 : (h + 1) * 128].astype(F32)
-        tab[pl.ds(h * 128, 128), :] = tt[...].T
+            tt[8 * t : 8 * t + 8, :] = acc[t]
+        tt[8 * 27 : 8 * 27 + 1, :] = jnp.where(cnt_ref[:, h * 128 : (h + 1) * 128] > 0, 1.0, 0.0)
+        tt[8 * 28 : 8 * 28 + 1, :] = edge_ref[:, h * 128 : (h + 1) * 128].astype(F32)
+        total = [tt[pl.ds(u, ROWS, stride=8), :] for u in range(8)]
+        while len(total) > 1:
+            total = [x + y for x, y in zip(total[::2], total[1::2])]
+        tab[pl.ds(h * 128, 128), :ROWS] = total[0].T
+    lane = lax.broadcasted_iota(jnp.int32, (n, 128), 1)
     for j in range(m1):
         row = tab[pl.ds(j * per_row, n, stride=slot), :]
         for k in range(1, per_row):
-            row = row + pltpu.roll(tab[pl.ds(j * per_row + k, n, stride=slot), :], ROWS * k, 1)
+            moved = pltpu.roll(tab[pl.ds(j * per_row + k, n, stride=slot), :], ROWS * k, 1)
+            row = jnp.where(lane < ROWS * k, row, moved)
         send1[:, j, :] = row
 
     @pl.when(is_mid)
@@ -515,8 +521,8 @@
             out_specs=(vm, vm),
             scratch_shapes=[
                 pltpu.VMEM((blocks // 128, 3, 3, 128, 128), F32),
-                pltpu.VMEM((9, 128, 128), F32),
-                pltpu.VMEM((128, 128), F32),
+                pltpu.VMEM((2, 9, 128, 128), F32),
+                pltpu.VMEM((8 * ROWS, 128), F32),
                 pltpu.VMEM((max(blocks, KEPT * edges), 128), F32),
                 pltpu.VMEM((n, m1, 128), F32),
                 pltpu.VMEM((n, KEPT, m1, 128), F32),

time: 16.8 us -> 16.2 us (0.964)
  Pallas kernels: 16.1 us -> 15.4 us
    pallas_call x1, Pallas kernels: 15.4 us -> 14.8 us  [on_device(): pl.pallas_call(functools.partial(kernel, (regions, pairs, blocks, edges,...]
where the time goes in v2:
time: 16.2 us; the launch traced here: 16 us
  Pallas kernels  15.4 us (95%)
  between operations  0.64 us (4%)
    pallas_call x1, Pallas kernels, on_device(): pl.pallas_call(functools.partial(kernel, (regions, pairs, blocks, edges,...  14.8 us
    pallas_call x1, Pallas kernels, on_device(): pl.pallas_call(finish, out_shape=(jax.ShapeDtypeStruct((6, edges), F32),...  0.62 us

profile of v2, /device:TPU:0, one launch (start us, length us, event | category | flops | bytes accessed | tf_op | source)
XLA Modules:
  0.0 16.0 jit_solution(5940452258544660662)
XLA Ops:
  0.6 14.8 %shard_map.95 = (f32[6,64]{1,0:T(8,128)S(1)}, f32[9,128]{1,0:T(8,128)S(1)}) custom-call(f32[3,256,128]{2,1,0:T(8,128)} %pts_hbm.1, f32[3,256,128]{2,1,0:T(8,128)} %off_hbm.1, f32[3,256,128]{2,1,0:T(8,128)} %nrm_hbm.1, s32[1,256]{1,0:T(1,128)} %bitcast.4, s32[1,256]{1,0:T(1,128)} %bitcast.5, s32[1,64]{1,0:T(1,128)} %bitcast.6, s32[1,64]{1,0:T(1,128)} %bitcast.7, ...), custom_call_target="tpu_custom_call" | custom-call | tf_op jit(solution)/shard_map/pallas_call | solution.py:517
  15.4 0.6 %shard_map.96 = (f32[6,64]{1,0:T(8,128)}, f32[9,128]{1,0:T(8,128)}) custom-call(f32[6,64]{1,0:T(8,128)S(1)} %get-tuple-element.4.pose_ref, f32[9,128]{1,0:T(8,128)S(1)} %get-tuple-element.5.rot_ref), custom_call_target="tpu_custom_call" | custom-call | tf_op jit(solution)/shard_map/pallas_call | solution.py:551

commit v3 on v2

--- a/solution.py
+++ b/solution.py
@@ -128,6 +128,7 @@
     per = edges // n
     per_row = 128 // ROWS
     m1 = slot * ROWS // 128
+    block = KEPT * m1
     ep = max(edges, 128)
     halves = blocks // 128
     reg, pair = lax.axis_index("region"), lax.axis_index("pair")
@@ -263,7 +264,7 @@
         for k in range(1, per_row):
             moved = pltpu.roll(tab[pl.ds(j * per_row + k, n, stride=slot), :], ROWS * k, 1)
             row = jnp.where(lane < ROWS * k, row, moved)
-        send1[:, j, :] = row
+        send1[pl.ds(j, n, stride=m1), :] = row
 
     @pl.when(is_mid)
     def _():
@@ -275,13 +276,16 @@
 
     each_mid(
         lambda k, where: pltpu.make_async_remote_copy(
-            send1.at[pl.ds(k * KEPT, KEPT)], recv1.at[me], s1, r1, device_id=where, device_id_type=MESH
+            send1.at[pl.ds(k * block, block)], recv1.at[pl.ds(pl.multiple_of(me * block, block), block)], s1, r1, device_id=where, device_id_type=MESH
         ).start()
     )
 
     @pl.when(is_mid)
     def _():
-        pltpu.make_async_copy(send1.at[pl.ds(rank * KEPT, KEPT)], recv1.at[me], r1).start()
+        pltpu.make_async_copy(
+            send1.at[pl.ds(pl.multiple_of(rank * block, block), block)],
+            recv1.at[pl.ds(pl.multiple_of(me * block, block), block)], r1,
+        ).start()
 
     for k in (-1, 1, -2, 2):
         where = (wrapped(reg + k % regions, regions), pair)
@@ -299,6 +303,86 @@
     pltpu.make_async_copy(scan_ref, sch.at[1], er).start()
     pltpu.make_async_copy(nbr_ref, nbh.at[1], nr).start()
 
+    pltpu.make_async_copy(rvh.at[pl.ds(0, 5)], rvh.at[pl.ds(0, 5)], hr).wait()
+    pltpu.make_async_copy(sch, sch, er).wait()
+    pltpu.make_async_copy(nbh, nbh, nr).wait()
+    for q in range(3):
+        near_tab[:, q * ep : q * ep + edges] = one_hot(nbh[q], 3 * scans, edges)
+        own_tab[:, q * ep : q * ep + edges] = one_hot(sch[q], scans, edges)
+        if ep > edges:
+            near_tab[:, q * ep + edges : (q + 1) * ep] = jnp.zeros((3 * scans, ep - edges), BF16)
+            own_tab[:, q * ep + edges : (q + 1) * ep] = jnp.zeros((scans, ep - edges), BF16)
+
+    def up(x, k):
+        return pltpu.roll(x, (8 - k) % 8, 0) if k % 8 else x
+
+    def picked(out, c, sets, width):
+        block = out[8 * c : 8 * c + 8]
+        if len(sets) == 1:
+            return block
+        value = block[:, :width]
+        for q in sets[1:]:
+            value = jnp.where(
+                lax.broadcasted_iota(jnp.int32, (8, width), 0) == q,
+                block[:, q * width : (q + 1) * width],
+                value,
+            )
+        return value
+
+    def between(rot, sets, shift):
+        cols = pl.ds(sets[0] * ep, len(sets) * ep)
+        parts = [
+            jnp.concatenate([up(x, s + shift) for x in rot], axis=0) for s in range(3)
+        ]
+        near = exact_dot(jnp.concatenate(parts, axis=1), near_tab[:, cols], ((1,), (0,)))
+        mine = exact_dot(parts[1], own_tab[:, cols], ((1,), (0,)))
+        return mat_tmul(
+            [picked(mine, c, sets, ep) for c in range(9)],
+            [picked(near, c, sets, ep) for c in range(9)],
+        )
+
+    def step(rot, link, relative, live, sets):
+        cols = pl.ds(sets[0] * ep, len(sets) * ep)
+        tangent = log_rotation(mat_mul(link, relative))
+        length = jnp.sqrt(tangent[0] * tangent[0] + tangent[1] * tangent[1] + tangent[2] * tangent[2])
+        weight = live / jnp.maximum(length, min_length)
+        weighed = jnp.concatenate([weight * x for x in tangent] + [weight], axis=0)
+        parts = [
+            exact_dot(weighed, own_tab[:, pl.ds(q * ep, ep)], ((1,), (1,))) for q in sets
+        ]
+        total = jnp.concatenate(parts, axis=1)
+        numer = [picked(total, c, sets, scans) for c in range(3)]
+        scale = 1.0 / (picked(total, 3, sets, scans) + 1.0)
+        return mat_mul(rot, exp_rotation([x * scale for x in numer]))
+
+    def padded(row):
+        if ep > edges:
+            row = jnp.concatenate([row, jnp.zeros((1, ep - edges), jnp.int32)], axis=1)
+        return jnp.broadcast_to(row, (8, ep))
+
+    own_lane, near_lane = padded(sch[1]), padded(nbh[1])
+    side = jnp.where(near_lane >= scans, 1, 0) + jnp.where(near_lane >= 2 * scans, 1, 0)
+    near_lane = near_lane - side * scans
+
+    def taken(x, index):
+        parts = [
+            jnp.take_along_axis(x, index[:, 128 * i : 128 * (i + 1)], axis=1, mode="promise_in_bounds")
+            for i in range(ep // 128)
+        ]
+        return jnp.concatenate(parts, axis=1) if len(parts) > 1 else parts[0]
+
+    def joined(rot):
+        near = []
+        for x in rot:
+            x = taken(x, near_lane)
+            near.append(jnp.where(side == 0, pltpu.roll(x, 1, 0), jnp.where(side == 1, x, pltpu.roll(x, 7, 0))))
+        return mat_tmul([taken(x, own_lane) for x in rot], near)
+
+    first = exp_rotation([rvh[:, c, :] for c in range(3)])
+    everyone = (0, 1, 2)
+    link = between(first, everyone, 0)
+    base = [up(x, 1) for x in first]
+
     @pl.when(is_mid)
     def _():
         pltpu.make_async_copy(recv1, recv1, r1).wait()
@@ -306,7 +390,7 @@
         span = wide // edges
         lanes = m1 * n
         for q in range(KEPT // span):
-            got = [recv1[:, q * span + h, j, :] for h in range(span) for j in range(m1)]
+            got = [recv1[pl.ds((q * span + h) * m1 + j, n, stride=block), :] for h in range(span) for j in range(m1)]
             got = jnp.concatenate(got, axis=0)
             turned_rows = [got[128 * i : 128 * (i + 1)].T for i in range(span * lanes // 128)]
             turned_rows = jnp.concatenate(turned_rows, axis=1) if len(turned_rows) > 1 else turned_rows[0]
@@ -380,72 +464,15 @@
                 part = edges // 128
                 count = 128 // per
                 for i in range(sets // held):
-                    block = tab[pl.ds(128 * i + j, count, stride=per), :]
+                    strip = tab[pl.ds(128 * i + j, count, stride=per), :]
                     for b in range(part):
-                        send2[pl.ds(b * count, count), j, i, :] = pltpu.roll(block, (128 - ROWS * b) % 128, 1)
+                        send2[pl.ds(b * count, count), j, i, :] = pltpu.roll(strip, (128 - ROWS * b) % 128, 1)
         each_other(
             lambda to, where: pltpu.make_async_remote_copy(
                 send2.at[to], recv2.at[rank], s2, r2, device_id=where, device_id_type=MESH
             ).start()
         )
         pltpu.make_async_copy(send2.at[me], recv2.at[rank], r2).start()
-
-    pltpu.make_async_copy(rvh.at[pl.ds(0, 5)], rvh.at[pl.ds(0, 5)], hr).wait()
-    pltpu.make_async_copy(sch, sch, er).wait()
-    pltpu.make_async_copy(nbh, nbh, nr).wait()
-    for q in range(3):
-        near_tab[:, q * ep : q * ep + edges] = one_hot(nbh[q], 3 * scans, edges)
-        own_tab[:, q * ep : q * ep + edges] = one_hot(sch[q], scans, edges)
-        if ep > edges:
-            near_tab[:, q * ep + edges : (q + 1) * ep] = jnp.zeros((3 * scans, ep - edges), BF16)
-            own_tab[:, q * ep + edges : (q + 1) * ep] = jnp.zeros((scans, ep - edges), BF16)
-
-    def up(x, k):
-        return pltpu.roll(x, (8 - k) % 8, 0) if k % 8 else x
-
-    def picked(out, c, sets, width):
-        block = out[8 * c : 8 * c + 8]
-        if len(sets) == 1:
-            return block
-        value = block[:, :width]
-        for q in sets[1:]:
-            value = jnp.where(
-                lax.broadcasted_iota(jnp.int32, (8, width), 0) == q,
-                block[:, q * width : (q + 1) * width],
-                value,
-            )
-        return value
-
-    def between(rot, sets, shift):
-        cols = pl.ds(sets[0] * ep, len(sets) * ep)
-        parts = [
-            jnp.concatenate([up(x, s + shift) for x in rot], axis=0) for s in range(3)
-        ]
-        near = exact_dot(jnp.concatenate(parts, axis=1), near_tab[:, cols], ((1,), (0,)))
-        mine = exact_dot(parts[1], own_tab[:, cols], ((1,), (0,)))
-        return mat_tmul(
-            [picked(mine, c, sets, ep) for c in range(9)],
-            [picked(near, c, sets, ep) for c in range(9)],
-        )
-
-    def step(rot, link, relative, live, sets):
-        cols = pl.ds(sets[0] * ep, len(sets) * ep)
-        tangent = log_rotation(mat_mul(link, relative))
-        length = jnp.sqrt(tangent[0] * tangent[0] + tangent[1] * tangent[1] + tangent[2] * tangent[2])
-        weight = live / jnp.maximum(length, min_length)
-        weighed = jnp.concatenate([weight * x for x in tangent] + [weight], axis=0)
-        parts = [
-            exact_dot(weighed, own_tab[:, pl.ds(q * ep, ep)], ((1,), (1,))) for q in sets
-        ]
-        total = jnp.concatenate(parts, axis=1)
-        numer = [picked(total, c, sets, scans) for c in range(3)]
-        scale = 1.0 / (picked(total, 3, sets, scans) + 1.0)
-        return mat_mul(rot, exp_rotation([x * scale for x in numer]))
-
-    first = exp_rotation([rvh[:, c, :] for c in range(3)])
-    everyone = (0, 1, 2)
-    link = between(first, everyone, 0)
-    base = [up(x, 1) for x in first]
 
     pltpu.make_async_copy(recv2, recv2, r2).wait()
     part = max(edges // 128, 1)
@@ -462,20 +489,20 @@
     back = jnp.concatenate(back, axis=1) if len(back) > 1 else back[0]
     comp = []
     for t in range(7):
-        block = back[8 * (t // 2) : 8 * (t // 2) + 8]
-        comp.append(pltpu.roll(block, 4, 0) if t % 2 else block)
+        tile = back[8 * (t // 2) : 8 * (t // 2) + 8]
+        comp.append(pltpu.roll(tile, 4, 0) if t % 2 else tile)
     for t in range(6):
         pose_ref[t : t + 1, :] = comp[t][1:2, :edges]
     relative = exp_rotation(comp[:3])
     second = step(base, link, relative, comp[6], everyone)
-    link = between(second, (1,), -1)
+    link = joined(second) if scans == 128 else between(second, (1,), -1)
     final = step(second, link, relative, comp[6], (1,))
     for c in range(9):
         rot_ref[c : c + 1, :] = final[c][1:2]
 
     @pl.when(is_mid)
     def _():
-        sent = send1.at[pl.ds(0, n - KEPT)]
+        sent = send1.at[pl.ds(0, n * m1 - block)]
         pltpu.make_async_copy(sent, sent, s1).wait()
         sent = send2.at[pl.ds(0, n - 1)]
         pltpu.make_async_copy(sent, sent, s2).wait()
@@ -524,8 +551,8 @@
                 pltpu.VMEM((2, 9, 128, 128), F32),
                 pltpu.VMEM((8 * ROWS, 128), F32),
                 pltpu.VMEM((max(blocks, KEPT * edges), 128), F32),
-                pltpu.VMEM((n, m1, 128), F32),
-                pltpu.VMEM((n, KEPT, m1, 128), F32),
+                pltpu.VMEM((n * m1, 128), F32),
+                pltpu.VMEM((n * KEPT * m1, 128), F32),
                 pltpu.VMEM((8 * ROWS, 128), F32),
                 pltpu.VMEM((3, 8 * sets, 128), F32),
                 pltpu.VMEM((sets, ROWS, 128), F32),

time: 16.2 us -> 16.1 us (level)
  no operation moved by 1% of the time
where the time goes in v3:
time: 16.1 us; the launch traced here: 15.9 us
  Pallas kernels  15.3 us (95%)
  between operations  0.64 us (4%)
    pallas_call x1, Pallas kernels, on_device(): pl.pallas_call(functools.partial(kernel, (regions, pairs, blocks, edges,...  14.6 us
    pallas_call x1, Pallas kernels, on_device(): pl.pallas_call(finish, out_shape=(jax.ShapeDtypeStruct((6, edges), F32),...  0.62 us

profile of v3, /device:TPU:0, one launch (start us, length us, event | category | flops | bytes accessed | tf_op | source)
XLA Modules:
  0.0 15.9 jit_solution(8613502817440619516)
XLA Ops:
  0.6 14.6 %shard_map.95 = (f32[6,64]{1,0:T(8,128)S(1)}, f32[9,128]{1,0:T(8,128)S(1)}) custom-call(f32[3,256,128]{2,1,0:T(8,128)} %pts_hbm.1, f32[3,256,128]{2,1,0:T(8,128)} %off_hbm.1, f32[3,256,128]{2,1,0:T(8,128)} %nrm_hbm.1, s32[1,256]{1,0:T(1,128)} %bitcast.4, s32[1,256]{1,0:T(1,128)} %bitcast.5, s32[1,64]{1,0:T(1,128)} %bitcast.6, s32[1,64]{1,0:T(1,128)} %bitcast.7, ...), custom_call_target="tpu_custom_call" | custom-call | tf_op jit(solution)/shard_map/pallas_call | solution.py:544
  15.3 0.6 %shard_map.96 = (f32[6,64]{1,0:T(8,128)}, f32[9,128]{1,0:T(8,128)}) custom-call(f32[6,64]{1,0:T(8,128)S(1)} %get-tuple-element.4.pose_ref, f32[9,128]{1,0:T(8,128)S(1)} %get-tuple-element.5.rot_ref), custom_call_target="tpu_custom_call" | custom-call | tf_op jit(solution)/shard_map/pallas_call | solution.py:578
